TPU v7x, 512 devices: a whole 4x4x16 slice. The times are simulated.
512 devices in a mesh: sta: 16 (over z), grp: 8 (over y, core), hr: 4 (over x).
Axes of the slice: x: 4, y: 4, z: 16, core: 2. Of those that a mesh axis runs over, the one named last changes fastest.
Arguments:
- spectra: bfloat16 [4, 128, 6, 8192], P('hr', 'sta'), may hold values from -6 to 6
- pair_source: int32 [2048], P(('sta', 'grp')), may hold values from 0 to 7
- pair_owner: int32 [2048, 1], P(('sta', 'grp')), may hold values from 0 to 15; in each aligned block of 16 rows (0 to 15, 16 to 31, ...) at most 2 rows name the same one
- pair_row: int32 [2048], P(('sta', 'grp')), may hold values from 0 to 7
Outputs:
- stacked: float32 [2048, 9, 1024], P(('sta', 'grp'))
Inputs may be any that keep to these rules, and one draw needn't show every extreme that they name: `pair_owner`: in each aligned block of 16 pairs (the pairs of one device) no value is named by more than 2 pairs, and in some block one value is named by exactly 2 pairs.
All inputs are finite; a program needn't handle non-finite values.
Results may differ from a plain program's by a relative error of at most 0.0032.
Values may be sent and summed in bfloat16 or wider, within the bound.
No kernel may reach another device: no remote copies, remote signals or barrier semaphores. Data moves between devices by JAX's collectives and lax.ppermute only.
A program may use at most 128 MiB of HBM per device.

v0:
```python
import math
import jax
import jax.numpy as jnp
from jax import lax
from jax.sharding import PartitionSpec as P

LAGS = 1024
two_pi = 2.0 * math.pi


def lag_table(start_bin, block_size, num_bins):
    bin_index = start_bin + jnp.arange(block_size, dtype=jnp.int32)
    lag_shift = jnp.arange(LAGS, dtype=jnp.int32) - LAGS // 2
    period = 2 * num_bins
    angles = jnp.mod(bin_index[:, None] * lag_shift[None, :], period).astype(jnp.float32) * (
        two_pi / period
    )
    return jnp.concatenate([jnp.cos(angles), -jnp.sin(angles)], axis=0).astype(jnp.bfloat16)


def cross_block(src_blk, rcv_blk):
    source_part = src_blk.astype(jnp.float32)
    recv_part = rcv_blk.astype(jnp.float32)
    src_re = source_part[..., 0:3, :][..., :, None, :]
    src_im = source_part[..., 3:6, :][..., :, None, :]
    rcv_re = recv_part[..., 0:3, :][..., None, :, :]
    rcv_im = recv_part[..., 3:6, :][..., None, :, :]
    cross_re = src_re * rcv_re + src_im * rcv_im
    cross_im = src_re * rcv_im - src_im * rcv_re
    return jnp.concatenate([cross_re, cross_im], axis=-1).astype(jnp.bfloat16)


def window_taper():
    lag_pos = jnp.arange(LAGS, dtype=jnp.float32)
    return 0.75 - 0.25 * jnp.cos(two_pi * (lag_pos + 0.5) / LAGS)


def slot_layout(owners, pair_row, peer_count, slot_cap):
    onehot = (owners[:, None] == jnp.arange(peer_count, dtype=jnp.int32)[None, :]).astype(jnp.int32)
    before = jnp.cumsum(onehot, axis=0) - onehot
    slot_rank = jnp.sum(before * onehot, axis=1)
    slot_index = owners * slot_cap + slot_rank
    request_table = jnp.zeros((peer_count * slot_cap,), jnp.int32).at[slot_index].set(pair_row)
    return (slot_index, request_table)


def body(spectra, pair_source, pair_owner, pair_row):
    hours_dev, sta_dev, comp_rows, num_bins = spectra.shape
    pair_count = pair_source.shape[0]
    owners = pair_owner[:, 0]
    peer_count = lax.axis_size("sta")
    slot_cap = 2 * pair_count // peer_count
    slot_index, request_table = slot_layout(owners, pair_row, peer_count, slot_cap)
    slot_owner = jnp.arange(peer_count * slot_cap, dtype=jnp.int32) // slot_cap
    wanted_station = slot_owner * sta_dev + request_table
    picked = jnp.take(lax.all_gather(spectra, "sta", axis=1, tiled=True), wanted_station, axis=1)
    receivers = jnp.take(picked, slot_index, axis=1)
    sources = jnp.take(spectra, pair_source, axis=1)
    block_size = min(512, num_bins)
    row_count = hours_dev * pair_count * 9

    def add_block(block_index, running):
        start_bin = (block_index * block_size).astype(jnp.int32)
        src_blk = lax.dynamic_slice_in_dim(sources, start_bin, block_size, 3)
        rcv_blk = lax.dynamic_slice_in_dim(receivers, start_bin, block_size, 3)
        cross = cross_block(src_blk, rcv_blk).reshape(row_count, 2 * block_size)
        table = lag_table(start_bin, block_size, num_bins)
        return running + jnp.dot(cross, table, preferred_element_type=jnp.float32)

    running = lax.fori_loop(
        0, num_bins // block_size, add_block, jnp.zeros((row_count, LAGS), jnp.float32)
    )
    local_sum = jnp.sum(running.reshape(hours_dev, pair_count, 9, LAGS), axis=0)
    stacked_sum = lax.psum(local_sum, "hr")
    hour_total = hours_dev * lax.axis_size("hr")
    return stacked_sum * window_taper()[None, None, :] / (hour_total * math.sqrt(num_bins))


def solution(mesh):
    placed = (
        P("hr", "sta", None, None),
        P(("sta", "grp")),
        P(("sta", "grp"), None),
        P(("sta", "grp")),
    )
    return jax.shard_map(
        body, mesh=mesh, in_specs=placed, out_specs=P(("sta", "grp"), None, None), check_vma=False
    )
```

profile of v0, /device:TPU:8, one launch (start us, length us, event | category | flops | bytes accessed | tf_op | source)
XLA Modules:
  0.0 459.1 jit_solution(4330169677160378186)
XLA Ops:
  10.8 151.2 %all-gather.2.cloned.1.call-done = bf16[1,128,6,8192]{3,1,2,0:T(8,128)(2,1)} async-done(((bf16[1,8,6,8192]{3,1,2,0:T(8,128)(2,1)}), bf16[1,128,6,8192]{3,1,2,0:T(8,128)(2,1)}) %all-gather.2.cloned.1.call-update) | async-done | bytes 12582928 | tf_op jit(solution)/shard_map/all_gather | solution.py:56
  161.9 13.8 %copy.16 = bf16[1,128,6,8192]{3,2,1,0:T(8,128)(2,1)} copy(bf16[1,128,6,8192]{3,1,2,0:T(8,128)(2,1)} %all-gather.2.cloned.1.call-done) | data formatting | bytes 25165824 | tf_op jit(solution)/shard_map/all_gather | solution.py:56
  175.7 8.5 %gather_fusion.1 = bf16[32,6,8192]{2,1,0:T(8,128)(2,1)} fusion(bf16[128,6,8192]{2,1,0:T(8,128)(2,1)} %bitcast.37, s32[1024]{0:T(1024)S(1)} %pad_clamp_fusion.1), kind=kCustom, calls=%fused_computation.1 | custom fusion | bytes 6291584 | tf_op jit(solution)/shard_map/jit(_take)/gather | solution.py:56
  184.2 4.7 %fusion.14 = bf16[32,6,8192]{2,1,0:T(8,128)(2,1)} fusion(bf16[32,6,8192]{2,1,0:T(8,128)(2,1)} %gather_fusion.1, pred[32]{0:T(512)(128)(4,1)S(1)} %get-tuple-element.143), kind=kLoop, calls=%fused_computation.35 | loop fusion | flops 1572864 | bytes 6291488 | tf_op jit(solution)/shard_map/jit(_take)/select_n | solution.py:56
  188.9 4.2 gather_fusion.2
  193.1 4.2 bitcast_select_fusion.1
  197.3 193.9 %while.16 = (s32[]{:T(128)}, f32[144,1024]{1,0:T(8,128)}, bf16[1,16,6,8192]{3,2,1,0:T(8,128)(2,1)}, bf16[1,16,6,8192]{3,2,1,0:T(8,128)(2,1)}, s32[]{:T(128)}, /*index=5*/s32[]{:T(128)}, s32[]{:T(128)}, s32[]{:T(128)}) while((s32[]{:T(128)}, f32[144,1024]{1,0:T(8,128)}, bf16[1,16,6,8192]{3,2,1,0:T(8,128)(2,1)}, ...), condition=%wide.region_4.5_spmd.clone, body=%wide.region_3.4_spmd.clone.sunk | while | flops 316671488 | bytes 13054157 | solution.py:70
  198.9 9.0 %cosine_convert_fusion.2 = (bf16[512,1024]{1,0:T(8,128)(2,1)S(1)}, bf16[512,1024]{1,0:T(8,128)(2,1)S(1)}) fusion(s32[1024]{0:T(1024)S(1)} %iota_add_fusion.4, s32[512]{0:T(512)S(1)} %iota_add_fusion.5), kind=kLoop, calls=%fused_computation.17.clone.1 | loop fusion | flops 8912896 | bytes 2103296 | tf_op jit(solution)/shard_map/convert
  211.1 9.0 %cosine_convert_fusion.2 = (bf16[512,1024]{1,0:T(8,128)(2,1)S(1)}, bf16[512,1024]{1,0:T(8,128)(2,1)S(1)}) fusion(s32[1024]{0:T(1024)S(1)} %iota_add_fusion.4, s32[512]{0:T(512)S(1)} %iota_add_fusion.5), kind=kLoop, calls=%fused_computation.17.clone.1 | loop fusion | flops 8912896 | bytes 2103296 | tf_op jit(solution)/shard_map/convert
  223.2 9.0 %cosine_convert_fusion.2 = (bf16[512,1024]{1,0:T(8,128)(2,1)S(1)}, bf16[512,1024]{1,0:T(8,128)(2,1)S(1)}) fusion(s32[1024]{0:T(1024)S(1)} %iota_add_fusion.4, s32[512]{0:T(512)S(1)} %iota_add_fusion.5), kind=kLoop, calls=%fused_computation.17.clone.1 | loop fusion | flops 8912896 | bytes 2103296 | tf_op jit(solution)/shard_map/convert
  235.3 9.0 %cosine_convert_fusion.2 = (bf16[512,1024]{1,0:T(8,128)(2,1)S(1)}, bf16[512,1024]{1,0:T(8,128)(2,1)S(1)}) fusion(s32[1024]{0:T(1024)S(1)} %iota_add_fusion.4, s32[512]{0:T(512)S(1)} %iota_add_fusion.5), kind=kLoop, calls=%fused_computation.17.clone.1 | loop fusion | flops 8912896 | bytes 2103296 | tf_op jit(solution)/shard_map/convert
  247.4 9.0 %cosine_convert_fusion.2 = (bf16[512,1024]{1,0:T(8,128)(2,1)S(1)}, bf16[512,1024]{1,0:T(8,128)(2,1)S(1)}) fusion(s32[1024]{0:T(1024)S(1)} %iota_add_fusion.4, s32[512]{0:T(512)S(1)} %iota_add_fusion.5), kind=kLoop, calls=%fused_computation.17.clone.1 | loop fusion | flops 8912896 | bytes 2103296 | tf_op jit(solution)/shard_map/convert
  259.5 9.0 %cosine_convert_fusion.2 = (bf16[512,1024]{1,0:T(8,128)(2,1)S(1)}, bf16[512,1024]{1,0:T(8,128)(2,1)S(1)}) fusion(s32[1024]{0:T(1024)S(1)} %iota_add_fusion.4, s32[512]{0:T(512)S(1)} %iota_add_fusion.5), kind=kLoop, calls=%fused_computation.17.clone.1 | loop fusion | flops 8912896 | bytes 2103296 | tf_op jit(solution)/shard_map/convert
  271.6 9.0 %cosine_convert_fusion.2 = (bf16[512,1024]{1,0:T(8,128)(2,1)S(1)}, bf16[512,1024]{1,0:T(8,128)(2,1)S(1)}) fusion(s32[1024]{0:T(1024)S(1)} %iota_add_fusion.4, s32[512]{0:T(512)S(1)} %iota_add_fusion.5), kind=kLoop, calls=%fused_computation.17.clone.1 | loop fusion | flops 8912896 | bytes 2103296 | tf_op jit(solution)/shard_map/convert
  283.8 9.0 %cosine_convert_fusion.2 = (bf16[512,1024]{1,0:T(8,128)(2,1)S(1)}, bf16[512,1024]{1,0:T(8,128)(2,1)S(1)}) fusion(s32[1024]{0:T(1024)S(1)} %iota_add_fusion.4, s32[512]{0:T(512)S(1)} %iota_add_fusion.5), kind=kLoop, calls=%fused_computation.17.clone.1 | loop fusion | flops 8912896 | bytes 2103296 | tf_op jit(solution)/shard_map/convert
  295.9 9.0 %cosine_convert_fusion.2 = (bf16[512,1024]{1,0:T(8,128)(2,1)S(1)}, bf16[512,1024]{1,0:T(8,128)(2,1)S(1)}) fusion(s32[1024]{0:T(1024)S(1)} %iota_add_fusion.4, s32[512]{0:T(512)S(1)} %iota_add_fusion.5), kind=kLoop, calls=%fused_computation.17.clone.1 | loop fusion | flops 8912896 | bytes 2103296 | tf_op jit(solution)/shard_map/convert
  308.0 9.0 %cosine_convert_fusion.2 = (bf16[512,1024]{1,0:T(8,128)(2,1)S(1)}, bf16[512,1024]{1,0:T(8,128)(2,1)S(1)}) fusion(s32[1024]{0:T(1024)S(1)} %iota_add_fusion.4, s32[512]{0:T(512)S(1)} %iota_add_fusion.5), kind=kLoop, calls=%fused_computation.17.clone.1 | loop fusion | flops 8912896 | bytes 2103296 | tf_op jit(solution)/shard_map/convert
  320.1 9.0 %cosine_convert_fusion.2 = (bf16[512,1024]{1,0:T(8,128)(2,1)S(1)}, bf16[512,1024]{1,0:T(8,128)(2,1)S(1)}) fusion(s32[1024]{0:T(1024)S(1)} %iota_add_fusion.4, s32[512]{0:T(512)S(1)} %iota_add_fusion.5), kind=kLoop, calls=%fused_computation.17.clone.1 | loop fusion | flops 8912896 | bytes 2103296 | tf_op jit(solution)/shard_map/convert
  332.2 9.0 %cosine_convert_fusion.2 = (bf16[512,1024]{1,0:T(8,128)(2,1)S(1)}, bf16[512,1024]{1,0:T(8,128)(2,1)S(1)}) fusion(s32[1024]{0:T(1024)S(1)} %iota_add_fusion.4, s32[512]{0:T(512)S(1)} %iota_add_fusion.5), kind=kLoop, calls=%fused_computation.17.clone.1 | loop fusion | flops 8912896 | bytes 2103296 | tf_op jit(solution)/shard_map/convert
  344.4 9.0 %cosine_convert_fusion.2 = (bf16[512,1024]{1,0:T(8,128)(2,1)S(1)}, bf16[512,1024]{1,0:T(8,128)(2,1)S(1)}) fusion(s32[1024]{0:T(1024)S(1)} %iota_add_fusion.4, s32[512]{0:T(512)S(1)} %iota_add_fusion.5), kind=kLoop, calls=%fused_computation.17.clone.1 | loop fusion | flops 8912896 | bytes 2103296 | tf_op jit(solution)/shard_map/convert
  356.5 9.0 %cosine_convert_fusion.2 = (bf16[512,1024]{1,0:T(8,128)(2,1)S(1)}, bf16[512,1024]{1,0:T(8,128)(2,1)S(1)}) fusion(s32[1024]{0:T(1024)S(1)} %iota_add_fusion.4, s32[512]{0:T(512)S(1)} %iota_add_fusion.5), kind=kLoop, calls=%fused_computation.17.clone.1 | loop fusion | flops 8912896 | bytes 2103296 | tf_op jit(solution)/shard_map/convert
  368.6 9.0 %cosine_convert_fusion.2 = (bf16[512,1024]{1,0:T(8,128)(2,1)S(1)}, bf16[512,1024]{1,0:T(8,128)(2,1)S(1)}) fusion(s32[1024]{0:T(1024)S(1)} %iota_add_fusion.4, s32[512]{0:T(512)S(1)} %iota_add_fusion.5), kind=kLoop, calls=%fused_computation.17.clone.1 | loop fusion | flops 8912896 | bytes 2103296 | tf_op jit(solution)/shard_map/convert
  380.7 9.0 %cosine_convert_fusion.2 = (bf16[512,1024]{1,0:T(8,128)(2,1)S(1)}, bf16[512,1024]{1,0:T(8,128)(2,1)S(1)}) fusion(s32[1024]{0:T(1024)S(1)} %iota_add_fusion.4, s32[512]{0:T(512)S(1)} %iota_add_fusion.5), kind=kLoop, calls=%fused_computation.17.clone.1 | loop fusion | flops 8912896 | bytes 2103296 | tf_op jit(solution)/shard_map/convert
  393.6 56.8 %all-reduce.2.cloned.1.call-done = f32[16,9,1024]{2,0,1:T(8,128)} async-done(((f32[16,9,1024]{2,0,1:T(8,128)}), f32[16,9,1024]{2,0,1:T(8,128)}) %all-reduce.2.cloned.1.call-update) | async-done | bytes 589840 | tf_op jit(solution)/shard_map/psum | solution.py:74
  (234 shorter events, 56.3 us)
Async XLA Ops:
  6.5 2.4 copy-start.2
  6.5 3.4 copy-start.3
  6.5 155.4 %all-gather.2.cloned.1.call-start = ((), (), s32[]{:S(2)}) async-start(), calls=%async_computation | async-start | bytes 13369344 | tf_op jit(solution)/shard_map/all_gather | solution.py:56
  7.3 443.1 %all-reduce.2.cloned.1.call-start = ((), (), s32[]{:S(2)}) async-start(), calls=%async_computation.1 | async-start | bytes 1179648 | tf_op jit(solution)/shard_map/psum | solution.py:74
  198.4 9.6 %copy-start = (f32[144,1024]{1,0:T(8,128)S(1)}, f32[144,1024]{1,0:T(8,128)}, u32[]{:S(2)}) copy-start(f32[144,1024]{1,0:T(8,128)} %get-tuple-element.211) | copy-start | bytes 1769476 | tf_op jit(solution)/shard_map/while
  210.5 9.6 %copy-start = (f32[144,1024]{1,0:T(8,128)S(1)}, f32[144,1024]{1,0:T(8,128)}, u32[]{:S(2)}) copy-start(f32[144,1024]{1,0:T(8,128)} %get-tuple-element.211) | copy-start | bytes 1769476 | tf_op jit(solution)/shard_map/while
  222.6 9.6 %copy-start = (f32[144,1024]{1,0:T(8,128)S(1)}, f32[144,1024]{1,0:T(8,128)}, u32[]{:S(2)}) copy-start(f32[144,1024]{1,0:T(8,128)} %get-tuple-element.211) | copy-start | bytes 1769476 | tf_op jit(solution)/shard_map/while
  234.7 9.6 %copy-start = (f32[144,1024]{1,0:T(8,128)S(1)}, f32[144,1024]{1,0:T(8,128)}, u32[]{:S(2)}) copy-start(f32[144,1024]{1,0:T(8,128)} %get-tuple-element.211) | copy-start | bytes 1769476 | tf_op jit(solution)/shard_map/while
  244.9 0.8 copy-start.1
  246.8 9.6 %copy-start = (f32[144,1024]{1,0:T(8,128)S(1)}, f32[144,1024]{1,0:T(8,128)}, u32[]{:S(2)}) copy-start(f32[144,1024]{1,0:T(8,128)} %get-tuple-element.211) | copy-start | bytes 1769476 | tf_op jit(solution)/shard_map/while
  257.0 0.8 copy-start.1
  259.0 9.6 %copy-start = (f32[144,1024]{1,0:T(8,128)S(1)}, f32[144,1024]{1,0:T(8,128)}, u32[]{:S(2)}) copy-start(f32[144,1024]{1,0:T(8,128)} %get-tuple-element.211) | copy-start | bytes 1769476 | tf_op jit(solution)/shard_map/while
  271.1 9.6 %copy-start = (f32[144,1024]{1,0:T(8,128)S(1)}, f32[144,1024]{1,0:T(8,128)}, u32[]{:S(2)}) copy-start(f32[144,1024]{1,0:T(8,128)} %get-tuple-element.211) | copy-start | bytes 1769476 | tf_op jit(solution)/shard_map/while
  283.2 9.6 %copy-start = (f32[144,1024]{1,0:T(8,128)S(1)}, f32[144,1024]{1,0:T(8,128)}, u32[]{:S(2)}) copy-start(f32[144,1024]{1,0:T(8,128)} %get-tuple-element.211) | copy-start | bytes 1769476 | tf_op jit(solution)/shard_map/while
  293.4 0.8 copy-start.1
  295.3 9.6 %copy-start = (f32[144,1024]{1,0:T(8,128)S(1)}, f32[144,1024]{1,0:T(8,128)}, u32[]{:S(2)}) copy-start(f32[144,1024]{1,0:T(8,128)} %get-tuple-element.211) | copy-start | bytes 1769476 | tf_op jit(solution)/shard_map/while
  305.5 0.8 copy-start.1
  307.4 9.6 %copy-start = (f32[144,1024]{1,0:T(8,128)S(1)}, f32[144,1024]{1,0:T(8,128)}, u32[]{:S(2)}) copy-start(f32[144,1024]{1,0:T(8,128)} %get-tuple-element.211) | copy-start | bytes 1769476 | tf_op jit(solution)/shard_map/while
  319.5 9.6 %copy-start = (f32[144,1024]{1,0:T(8,128)S(1)}, f32[144,1024]{1,0:T(8,128)}, u32[]{:S(2)}) copy-start(f32[144,1024]{1,0:T(8,128)} %get-tuple-element.211) | copy-start | bytes 1769476 | tf_op jit(solution)/shard_map/while
  331.7 9.6 %copy-start = (f32[144,1024]{1,0:T(8,128)S(1)}, f32[144,1024]{1,0:T(8,128)}, u32[]{:S(2)}) copy-start(f32[144,1024]{1,0:T(8,128)} %get-tuple-element.211) | copy-start | bytes 1769476 | tf_op jit(solution)/shard_map/while
  343.8 9.6 %copy-start = (f32[144,1024]{1,0:T(8,128)S(1)}, f32[144,1024]{1,0:T(8,128)}, u32[]{:S(2)}) copy-start(f32[144,1024]{1,0:T(8,128)} %get-tuple-element.211) | copy-start | bytes 1769476 | tf_op jit(solution)/shard_map/while
  355.9 9.6 %copy-start = (f32[144,1024]{1,0:T(8,128)S(1)}, f32[144,1024]{1,0:T(8,128)}, u32[]{:S(2)}) copy-start(f32[144,1024]{1,0:T(8,128)} %get-tuple-element.211) | copy-start | bytes 1769476 | tf_op jit(solution)/shard_map/while
  368.0 9.6 %copy-start = (f32[144,1024]{1,0:T(8,128)S(1)}, f32[144,1024]{1,0:T(8,128)}, u32[]{:S(2)}) copy-start(f32[144,1024]{1,0:T(8,128)} %get-tuple-element.211) | copy-start | bytes 1769476 | tf_op jit(solution)/shard_map/while
  380.1 9.6 %copy-start = (f32[144,1024]{1,0:T(8,128)S(1)}, f32[144,1024]{1,0:T(8,128)}, u32[]{:S(2)}) copy-start(f32[144,1024]{1,0:T(8,128)} %get-tuple-element.211) | copy-start | bytes 1769476 | tf_op jit(solution)/shard_map/while
  (12 other events, 9.8 us)
Sparse Core Ops, SparseCore 0:
  9.4 152.4 all-gather.1
  393.6 56.6 all-reduce.1
where the time goes:
time: 460 us; the launch traced here: 459 us
  waiting for transfers between devices  209 us (45%)
  other arithmetic  176 us (38%)
  local copies, waits for them, and re-layouts  50.5 us (11%)
  between operations  13.5 us (3%)
  matrix products  9.22 us (2%)
    all_gather x1, waiting for transfers between devices, body(): lax.all_gather(spectra, 'sta', axis=1, tiled=True)  151 us
    another operation x32, other arithmetic  148 us
    psum x1, waiting for transfers between devices, body(): stacked_sum = lax.psum(local_sum, 'hr')  56.8 us
    convert_element_type x16, other arithmetic, cross_block(): recv_part = rcv_blk.astype(jnp.float32)  16.4 us
    all_gather x1, local copies, waits for them, and re-layouts, body(): lax.all_gather(spectra, 'sta', axis=1, tiled=True)  13.8 us
    while x64, local copies, waits for them, and re-layouts  13 us
    dot_general x16, matrix products, add_block(): return running + jnp.dot(cross, table, preferred_element_type=jnp.float32)  9.22 us
  transfers between devices with their start and end apart: 2, of which 2 were waited for; matrix products, arithmetic and copies ran while one was open for 1% of the time, Pallas kernels for 0%

commit v1 on v0

--- a/solution.py
+++ b/solution.py
@@ -71,7 +71,7 @@
         0, num_bins // block_size, add_block, jnp.zeros((row_count, LAGS), jnp.float32)
     )
     local_sum = jnp.sum(running.reshape(hours_dev, pair_count, 9, LAGS), axis=0)
-    stacked_sum = lax.psum(local_sum, "hr")
+    stacked_sum = jnp.sum(lax.all_gather(local_sum, "hr"), axis=0)
     hour_total = hours_dev * lax.axis_size("hr")
     return stacked_sum * window_taper()[None, None, :] / (hour_total * math.sqrt(num_bins))
 

time: 460 us -> 443 us (0.963)
  the two profiles are of different devices: /device:TPU:8 before, /device:TPU:1 now
where the time goes in v1:
time: 443 us
  waiting for transfers between devices  192 us (43%)
  other arithmetic  176 us (40%)
  local copies, waits for them, and re-layouts  50.5 us (11%)
  between operations  13.5 us (3%)
  matrix products  9.22 us (2%)
    all_gather x1, waiting for transfers between devices, body(): lax.all_gather(spectra, 'sta', axis=1, tiled=True)  152 us
    another operation x32, other arithmetic  148 us
    all_gather x1, waiting for transfers between devices, body(): stacked_sum = jnp.sum(lax.all_gather(local_sum, 'hr'), axis=0)  38.7 us
    convert_element_type x16, other arithmetic, cross_block(): recv_part = rcv_blk.astype(jnp.float32)  16.4 us
    all_gather x1, local copies, waits for them, and re-layouts, body(): lax.all_gather(spectra, 'sta', axis=1, tiled=True)  13.8 us
    while x64, local copies, waits for them, and re-layouts  13 us
    dot_general x16, matrix products, add_block(): return running + jnp.dot(cross, table, preferred_element_type=jnp.float32)  9.22 us
  transfers between devices with their start and end apart: 2, of which 2 were waited for; matrix products, arithmetic and copies ran while one was open for 1% of the time, Pallas kernels for 0%

profile of v1, /device:TPU:1, one launch (start us, length us, event | category | flops | bytes accessed | tf_op | source)
XLA Modules:
  0.0 442.8 jit_solution(776290719901123749)
XLA Ops:
  10.8 152.1 %all-gather.3.cloned.1.call-done = bf16[1,128,6,8192]{3,1,2,0:T(8,128)(2,1)} async-done(((bf16[1,8,6,8192]{3,1,2,0:T(8,128)(2,1)}), bf16[1,128,6,8192]{3,1,2,0:T(8,128)(2,1)}) %all-gather.3.cloned.1.call-update) | async-done | bytes 12582928 | tf_op jit(solution)/shard_map/all_gather | solution.py:56
  162.8 13.8 %copy.20 = bf16[1,128,6,8192]{3,2,1,0:T(8,128)(2,1)} copy(bf16[1,128,6,8192]{3,1,2,0:T(8,128)(2,1)} %all-gather.3.cloned.1.call-done) | data formatting | bytes 25165824 | tf_op jit(solution)/shard_map/all_gather | solution.py:56
  176.6 8.5 %gather_fusion.1 = bf16[32,6,8192]{2,1,0:T(8,128)(2,1)} fusion(bf16[128,6,8192]{2,1,0:T(8,128)(2,1)} %bitcast.37, s32[1024]{0:T(1024)S(1)} %pad_clamp_fusion.1), kind=kCustom, calls=%fused_computation.1 | custom fusion | bytes 6291584 | tf_op jit(solution)/shard_map/jit(_take)/gather | solution.py:56
  185.1 4.7 %fusion.14 = bf16[32,6,8192]{2,1,0:T(8,128)(2,1)} fusion(bf16[32,6,8192]{2,1,0:T(8,128)(2,1)} %gather_fusion.1, pred[32]{0:T(512)(128)(4,1)S(1)} %get-tuple-element.143), kind=kLoop, calls=%fused_computation.35 | loop fusion | flops 1572864 | bytes 6291488 | tf_op jit(solution)/shard_map/jit(_take)/select_n | solution.py:56
  189.8 4.2 gather_fusion.2
  194.0 4.2 bitcast_select_fusion.1
  198.1 193.9 %while.16 = (s32[]{:T(128)}, f32[144,1024]{1,0:T(8,128)}, bf16[1,16,6,8192]{3,2,1,0:T(8,128)(2,1)}, bf16[1,16,6,8192]{3,2,1,0:T(8,128)(2,1)}, s32[]{:T(128)}, /*index=5*/s32[]{:T(128)}, s32[]{:T(128)}, s32[]{:T(128)}) while((s32[]{:T(128)}, f32[144,1024]{1,0:T(8,128)}, bf16[1,16,6,8192]{3,2,1,0:T(8,128)(2,1)}, ...), condition=%wide.region_4.5_spmd.clone, body=%wide.region_3.4_spmd.clone.sunk | while | flops 316671488 | bytes 13054157 | solution.py:70
  199.8 9.0 %cosine_convert_fusion.2 = (bf16[512,1024]{1,0:T(8,128)(2,1)S(1)}, bf16[512,1024]{1,0:T(8,128)(2,1)S(1)}) fusion(s32[1024]{0:T(1024)S(1)} %iota_add_fusion.4, s32[512]{0:T(512)S(1)} %iota_add_fusion.5), kind=kLoop, calls=%fused_computation.17.clone.1 | loop fusion | flops 8912896 | bytes 2103296 | tf_op jit(solution)/shard_map/convert
  211.9 9.0 %cosine_convert_fusion.2 = (bf16[512,1024]{1,0:T(8,128)(2,1)S(1)}, bf16[512,1024]{1,0:T(8,128)(2,1)S(1)}) fusion(s32[1024]{0:T(1024)S(1)} %iota_add_fusion.4, s32[512]{0:T(512)S(1)} %iota_add_fusion.5), kind=kLoop, calls=%fused_computation.17.clone.1 | loop fusion | flops 8912896 | bytes 2103296 | tf_op jit(solution)/shard_map/convert
  224.1 9.0 %cosine_convert_fusion.2 = (bf16[512,1024]{1,0:T(8,128)(2,1)S(1)}, bf16[512,1024]{1,0:T(8,128)(2,1)S(1)}) fusion(s32[1024]{0:T(1024)S(1)} %iota_add_fusion.4, s32[512]{0:T(512)S(1)} %iota_add_fusion.5), kind=kLoop, calls=%fused_computation.17.clone.1 | loop fusion | flops 8912896 | bytes 2103296 | tf_op jit(solution)/shard_map/convert
  236.2 9.0 %cosine_convert_fusion.2 = (bf16[512,1024]{1,0:T(8,128)(2,1)S(1)}, bf16[512,1024]{1,0:T(8,128)(2,1)S(1)}) fusion(s32[1024]{0:T(1024)S(1)} %iota_add_fusion.4, s32[512]{0:T(512)S(1)} %iota_add_fusion.5), kind=kLoop, calls=%fused_computation.17.clone.1 | loop fusion | flops 8912896 | bytes 2103296 | tf_op jit(solution)/shard_map/convert
  248.3 9.0 %cosine_convert_fusion.2 = (bf16[512,1024]{1,0:T(8,128)(2,1)S(1)}, bf16[512,1024]{1,0:T(8,128)(2,1)S(1)}) fusion(s32[1024]{0:T(1024)S(1)} %iota_add_fusion.4, s32[512]{0:T(512)S(1)} %iota_add_fusion.5), kind=kLoop, calls=%fused_computation.17.clone.1 | loop fusion | flops 8912896 | bytes 2103296 | tf_op jit(solution)/shard_map/convert
  260.4 9.0 %cosine_convert_fusion.2 = (bf16[512,1024]{1,0:T(8,128)(2,1)S(1)}, bf16[512,1024]{1,0:T(8,128)(2,1)S(1)}) fusion(s32[1024]{0:T(1024)S(1)} %iota_add_fusion.4, s32[512]{0:T(512)S(1)} %iota_add_fusion.5), kind=kLoop, calls=%fused_computation.17.clone.1 | loop fusion | flops 8912896 | bytes 2103296 | tf_op jit(solution)/shard_map/convert
  272.5 9.0 %cosine_convert_fusion.2 = (bf16[512,1024]{1,0:T(8,128)(2,1)S(1)}, bf16[512,1024]{1,0:T(8,128)(2,1)S(1)}) fusion(s32[1024]{0:T(1024)S(1)} %iota_add_fusion.4, s32[512]{0:T(512)S(1)} %iota_add_fusion.5), kind=kLoop, calls=%fused_computation.17.clone.1 | loop fusion | flops 8912896 | bytes 2103296 | tf_op jit(solution)/shard_map/convert
  284.6 9.0 %cosine_convert_fusion.2 = (bf16[512,1024]{1,0:T(8,128)(2,1)S(1)}, bf16[512,1024]{1,0:T(8,128)(2,1)S(1)}) fusion(s32[1024]{0:T(1024)S(1)} %iota_add_fusion.4, s32[512]{0:T(512)S(1)} %iota_add_fusion.5), kind=kLoop, calls=%fused_computation.17.clone.1 | loop fusion | flops 8912896 | bytes 2103296 | tf_op jit(solution)/shard_map/convert
  296.8 9.0 %cosine_convert_fusion.2 = (bf16[512,1024]{1,0:T(8,128)(2,1)S(1)}, bf16[512,1024]{1,0:T(8,128)(2,1)S(1)}) fusion(s32[1024]{0:T(1024)S(1)} %iota_add_fusion.4, s32[512]{0:T(512)S(1)} %iota_add_fusion.5), kind=kLoop, calls=%fused_computation.17.clone.1 | loop fusion | flops 8912896 | bytes 2103296 | tf_op jit(solution)/shard_map/convert
  308.9 9.0 %cosine_convert_fusion.2 = (bf16[512,1024]{1,0:T(8,128)(2,1)S(1)}, bf16[512,1024]{1,0:T(8,128)(2,1)S(1)}) fusion(s32[1024]{0:T(1024)S(1)} %iota_add_fusion.4, s32[512]{0:T(512)S(1)} %iota_add_fusion.5), kind=kLoop, calls=%fused_computation.17.clone.1 | loop fusion | flops 8912896 | bytes 2103296 | tf_op jit(solution)/shard_map/convert
  321.0 9.0 %cosine_convert_fusion.2 = (bf16[512,1024]{1,0:T(8,128)(2,1)S(1)}, bf16[512,1024]{1,0:T(8,128)(2,1)S(1)}) fusion(s32[1024]{0:T(1024)S(1)} %iota_add_fusion.4, s32[512]{0:T(512)S(1)} %iota_add_fusion.5), kind=kLoop, calls=%fused_computation.17.clone.1 | loop fusion | flops 8912896 | bytes 2103296 | tf_op jit(solution)/shard_map/convert
  333.1 9.0 %cosine_convert_fusion.2 = (bf16[512,1024]{1,0:T(8,128)(2,1)S(1)}, bf16[512,1024]{1,0:T(8,128)(2,1)S(1)}) fusion(s32[1024]{0:T(1024)S(1)} %iota_add_fusion.4, s32[512]{0:T(512)S(1)} %iota_add_fusion.5), kind=kLoop, calls=%fused_computation.17.clone.1 | loop fusion | flops 8912896 | bytes 2103296 | tf_op jit(solution)/shard_map/convert
  345.2 9.0 %cosine_convert_fusion.2 = (bf16[512,1024]{1,0:T(8,128)(2,1)S(1)}, bf16[512,1024]{1,0:T(8,128)(2,1)S(1)}) fusion(s32[1024]{0:T(1024)S(1)} %iota_add_fusion.4, s32[512]{0:T(512)S(1)} %iota_add_fusion.5), kind=kLoop, calls=%fused_computation.17.clone.1 | loop fusion | flops 8912896 | bytes 2103296 | tf_op jit(solution)/shard_map/convert
  357.3 9.0 %cosine_convert_fusion.2 = (bf16[512,1024]{1,0:T(8,128)(2,1)S(1)}, bf16[512,1024]{1,0:T(8,128)(2,1)S(1)}) fusion(s32[1024]{0:T(1024)S(1)} %iota_add_fusion.4, s32[512]{0:T(512)S(1)} %iota_add_fusion.5), kind=kLoop, calls=%fused_computation.17.clone.1 | loop fusion | flops 8912896 | bytes 2103296 | tf_op jit(solution)/shard_map/convert
  369.5 9.0 %cosine_convert_fusion.2 = (bf16[512,1024]{1,0:T(8,128)(2,1)S(1)}, bf16[512,1024]{1,0:T(8,128)(2,1)S(1)}) fusion(s32[1024]{0:T(1024)S(1)} %iota_add_fusion.4, s32[512]{0:T(512)S(1)} %iota_add_fusion.5), kind=kLoop, calls=%fused_computation.17.clone.1 | loop fusion | flops 8912896 | bytes 2103296 | tf_op jit(solution)/shard_map/convert
  381.6 9.0 %cosine_convert_fusion.2 = (bf16[512,1024]{1,0:T(8,128)(2,1)S(1)}, bf16[512,1024]{1,0:T(8,128)(2,1)S(1)}) fusion(s32[1024]{0:T(1024)S(1)} %iota_add_fusion.4, s32[512]{0:T(512)S(1)} %iota_add_fusion.5), kind=kLoop, calls=%fused_computation.17.clone.1 | loop fusion | flops 8912896 | bytes 2103296 | tf_op jit(solution)/shard_map/convert
  394.4 38.7 %all-gather.5.cloned.1.call-done = f32[4,16,9,1024]{3,1,2,0:T(8,128)} async-done(((f32[1,16,9,1024]{3,1,2,0:T(8,128)}), f32[4,16,9,1024]{3,1,2,0:T(8,128)}) %all-gather.5.cloned.1.call-update) | async-done | bytes 2359312 | tf_op jit(solution)/shard_map/all_gather | solution.py:74
  (235 shorter events, 57.1 us)
Async XLA Ops:
  6.5 2.4 copy-start.2
  6.5 3.4 copy-start.3
  6.5 156.3 %all-gather.3.cloned.1.call-start = ((), (), s32[]{:S(2)}) async-start(), calls=%async_computation | async-start | bytes 13369344 | tf_op jit(solution)/shard_map/all_gather | solution.py:56
  7.3 425.9 %all-gather.5.cloned.1.call-start = ((), (), s32[]{:S(2)}) async-start(), calls=%async_computation.1 | async-start | bytes 2949120 | tf_op jit(solution)/shard_map/all_gather | solution.py:74
  199.2 9.6 %copy-start = (f32[144,1024]{1,0:T(8,128)S(1)}, f32[144,1024]{1,0:T(8,128)}, u32[]{:S(2)}) copy-start(f32[144,1024]{1,0:T(8,128)} %get-tuple-element.211) | copy-start | bytes 1769476 | tf_op jit(solution)/shard_map/while
  211.4 9.6 %copy-start = (f32[144,1024]{1,0:T(8,128)S(1)}, f32[144,1024]{1,0:T(8,128)}, u32[]{:S(2)}) copy-start(f32[144,1024]{1,0:T(8,128)} %get-tuple-element.211) | copy-start | bytes 1769476 | tf_op jit(solution)/shard_map/while
  221.6 0.8 copy-start.1
  223.5 9.6 %copy-start = (f32[144,1024]{1,0:T(8,128)S(1)}, f32[144,1024]{1,0:T(8,128)}, u32[]{:S(2)}) copy-start(f32[144,1024]{1,0:T(8,128)} %get-tuple-element.211) | copy-start | bytes 1769476 | tf_op jit(solution)/shard_map/while
  233.7 0.8 copy-start.1
  235.6 9.6 %copy-start = (f32[144,1024]{1,0:T(8,128)S(1)}, f32[144,1024]{1,0:T(8,128)}, u32[]{:S(2)}) copy-start(f32[144,1024]{1,0:T(8,128)} %get-tuple-element.211) | copy-start | bytes 1769476 | tf_op jit(solution)/shard_map/while
  247.7 9.6 %copy-start = (f32[144,1024]{1,0:T(8,128)S(1)}, f32[144,1024]{1,0:T(8,128)}, u32[]{:S(2)}) copy-start(f32[144,1024]{1,0:T(8,128)} %get-tuple-element.211) | copy-start | bytes 1769476 | tf_op jit(solution)/shard_map/while
  259.8 9.6 %copy-start = (f32[144,1024]{1,0:T(8,128)S(1)}, f32[144,1024]{1,0:T(8,128)}, u32[]{:S(2)}) copy-start(f32[144,1024]{1,0:T(8,128)} %get-tuple-element.211) | copy-start | bytes 1769476 | tf_op jit(solution)/shard_map/while
  270.0 0.8 copy-start.1
  271.9 9.6 %copy-start = (f32[144,1024]{1,0:T(8,128)S(1)}, f32[144,1024]{1,0:T(8,128)}, u32[]{:S(2)}) copy-start(f32[144,1024]{1,0:T(8,128)} %get-tuple-element.211) | copy-start | bytes 1769476 | tf_op jit(solution)/shard_map/while
  284.1 9.6 %copy-start = (f32[144,1024]{1,0:T(8,128)S(1)}, f32[144,1024]{1,0:T(8,128)}, u32[]{:S(2)}) copy-start(f32[144,1024]{1,0:T(8,128)} %get-tuple-element.211) | copy-start | bytes 1769476 | tf_op jit(solution)/shard_map/while
  296.2 9.6 %copy-start = (f32[144,1024]{1,0:T(8,128)S(1)}, f32[144,1024]{1,0:T(8,128)}, u32[]{:S(2)}) copy-start(f32[144,1024]{1,0:T(8,128)} %get-tuple-element.211) | copy-start | bytes 1769476 | tf_op jit(solution)/shard_map/while
  308.3 9.6 %copy-start = (f32[144,1024]{1,0:T(8,128)S(1)}, f32[144,1024]{1,0:T(8,128)}, u32[]{:S(2)}) copy-start(f32[144,1024]{1,0:T(8,128)} %get-tuple-element.211) | copy-start | bytes 1769476 | tf_op jit(solution)/shard_map/while
  318.5 0.8 copy-start.1
  320.4 9.6 %copy-start = (f32[144,1024]{1,0:T(8,128)S(1)}, f32[144,1024]{1,0:T(8,128)}, u32[]{:S(2)}) copy-start(f32[144,1024]{1,0:T(8,128)} %get-tuple-element.211) | copy-start | bytes 1769476 | tf_op jit(solution)/shard_map/while
  332.5 9.6 %copy-start = (f32[144,1024]{1,0:T(8,128)S(1)}, f32[144,1024]{1,0:T(8,128)}, u32[]{:S(2)}) copy-start(f32[144,1024]{1,0:T(8,128)} %get-tuple-element.211) | copy-start | bytes 1769476 | tf_op jit(solution)/shard_map/while
  344.7 9.6 %copy-start = (f32[144,1024]{1,0:T(8,128)S(1)}, f32[144,1024]{1,0:T(8,128)}, u32[]{:S(2)}) copy-start(f32[144,1024]{1,0:T(8,128)} %get-tuple-element.211) | copy-start | bytes 1769476 | tf_op jit(solution)/shard_map/while
  356.8 9.6 %copy-start = (f32[144,1024]{1,0:T(8,128)S(1)}, f32[144,1024]{1,0:T(8,128)}, u32[]{:S(2)}) copy-start(f32[144,1024]{1,0:T(8,128)} %get-tuple-element.211) | copy-start | bytes 1769476 | tf_op jit(solution)/shard_map/while
  368.9 9.6 %copy-start = (f32[144,1024]{1,0:T(8,128)S(1)}, f32[144,1024]{1,0:T(8,128)}, u32[]{:S(2)}) copy-start(f32[144,1024]{1,0:T(8,128)} %get-tuple-element.211) | copy-start | bytes 1769476 | tf_op jit(solution)/shard_map/while
  381.0 9.6 %copy-start = (f32[144,1024]{1,0:T(8,128)S(1)}, f32[144,1024]{1,0:T(8,128)}, u32[]{:S(2)}) copy-start(f32[144,1024]{1,0:T(8,128)} %get-tuple-element.211) | copy-start | bytes 1769476 | tf_op jit(solution)/shard_map/while
  (12 other events, 9.8 us)
Sparse Core Ops, SparseCore 0:
  9.4 153.3 all-gather.2
  394.5 38.6 all-gather.4
